TPU v7x, 512 devices: a whole 4x4x16 slice. The times are simulated.
512 devices in a mesh: blk: 32 (over z, core), ctr: 16 (over x, y).
Axes of the slice: x: 4, y: 4, z: 16, core: 2. Of those that a mesh axis runs over, the one named last changes fastest.
Arguments:
- integrals: float32 [32, 800, 12800], P('blk', None, 'ctr'), may hold values from -0.078125 to 0.078125
- amplitudes: float32 [8, 12800, 128], P(None, 'ctr', 'blk'), may hold values from -6 to 6
- blockmap: int32 [32], replicated, may hold values from 0 to 31, each once
- vir_energy: float32 [320], replicated, may hold values from 0.2 to 3
- occ_energy: float32 [32], replicated, may hold values from -2 to -0.3
Outputs:
- ladder: float32 [32, 800, 128], P('blk', 'ctr')
- increment: float32 [32, 800, 128], P('blk', 'ctr')
Inputs may be any that keep to these rules, and one draw needn't show every extreme that they name: `blockmap`: every block number appears in exactly one slot.
All inputs are finite; a program needn't handle non-finite values.
Results may differ from a plain program's by a relative error of at most 0.0003.
Values sent between devices are 32-bit elements; how exact they have to be, the bound alone decides.
A program may use at most 64 MiB of HBM per device.

v0:
```python
import jax
import jax.numpy as jnp
from jax import lax
from jax.sharding import PartitionSpec as P

NIRR = 8
VI = 40
OI = 4


def denominator(block, groups, ab_block, start, count, columns, vir_energy, occ_energy):
    irrep = block // groups
    rows = block % groups * ab_block + start + jnp.arange(count, dtype=jnp.int32)
    arow = rows // (VI * VI)
    first = arow * VI + rows // VI % VI
    second = jnp.bitwise_xor(arow, irrep) * VI + rows % VI
    cols = jnp.arange(columns, dtype=jnp.int32)
    orow = cols // (OI * OI)
    hole_one = orow * OI + cols // OI % OI
    hole_two = jnp.bitwise_xor(orow, irrep) * OI + cols % OI
    upper = jnp.take(vir_energy, first) + jnp.take(vir_energy, second)
    lower = jnp.take(occ_energy, hole_one) + jnp.take(occ_energy, hole_two)
    return upper[:, None] - lower[None, :]


def on_device(integrals, amplitudes, blockmap, vir_energy, occ_energy):
    blocks = lax.axis_size("blk")
    groups = blocks // NIRR
    block = blockmap[lax.axis_index("blk")]
    irrep = block // groups
    local = integrals[0]
    ab_block = local.shape[0]
    share = ab_block // lax.axis_size("ctr")
    chosen = lax.dynamic_index_in_dim(
        lax.all_gather(amplitudes, "blk", axis=2, tiled=True), irrep, 0, keepdims=False
    )
    partial_value = jnp.dot(
        local, chosen, preferred_element_type=jnp.float32, precision=lax.Precision.HIGHEST
    )
    offset = lax.axis_index("ctr") * share
    summed = lax.psum(partial_value, "ctr")
    mine = lax.dynamic_slice_in_dim(summed, offset, share, 0)
    denom = denominator(
        block, groups, ab_block, offset, share, partial_value.shape[1], vir_energy, occ_energy
    )
    return (mine[None], (mine / denom)[None])


def solution(mesh):
    placed = (P("blk", None, "ctr"), P(None, "ctr", "blk"), P(), P(), P())
    return jax.shard_map(
        on_device,
        mesh=mesh,
        in_specs=placed,
        out_specs=(P("blk", "ctr", None), P("blk", "ctr", None)),
        check_vma=False,
    )
```

profile of v0, /device:TPU:32, one launch (start us, length us, event | category | flops | bytes accessed | tf_op | source)
XLA Modules:
  0.0 216.9 jit_solution(8008306709315105640)
XLA Ops:
  7.2 0.0 copy-start
  7.2 0.0 all-gather.2.cloned.1.call-start
  7.2 1.7 copy.11
  8.9 0.0 all-gather.2.cloned.1.call-update
  9.0 0.0 all-reduce.2.cloned.1.call-start
  9.0 1.2 dynamic_slice.10
  12.9 1.5 gather_fusion
  14.4 1.5 gather_fusion.1
  15.9 1.6 gather_fusion.3
  17.5 1.6 gather_fusion.2
  19.1 68.6 %all-gather.2.cloned.1.call-done = f32[8,800,128]{1,0,2:T(8,128)} async-done(((f32[8,800,4]{1,0,2:T(8,128)}), f32[8,800,128]{1,0,2:T(8,128)}) %all-gather.2.cloned.1.call-update) | async-done | bytes 3276816 | tf_op jit(solution)/shard_map/all_gather | solution.py:35
  87.7 2.4 %constant_dynamic-slice_fusion.1 = f32[1,800,128]{1,0,2:T(1,128)S(1)} fusion(f32[8,800,128]{1,0,2:T(8,128)} %all-gather.2.cloned.1.call-done, s32[]{:T(128)S(6)} %select_n.74), kind=kLoop, calls=%fused_computation.47 | loop fusion | bytes 819204 | tf_op jit(solution)/shard_map/jit(dynamic_index_in_dim)/dynamic_slice | solution.py:34
  90.1 1.1 copy.14
  91.2 0.0 copy-done
  91.2 4.2 %fusion.2 = f32[800,128]{1,0:T(8,128)} fusion(f32[1,800,800]{2,1,0:T(8,128)S(1)} %copy-done, f32[1,800,128]{2,1,0:T(8,128)} %copy.14), kind=kOutput, calls=%fused_computation.6 | convolution fusion | flops 983040000 | bytes 3379200 | tf_op jit(solution)/shard_map/dot_general | solution.py:37
  95.4 0.0 all-reduce.2.cloned.1.call-update
  95.5 112.5 %all-reduce.2.cloned.1.call-done = f32[800,128]{1,0:T(8,128)} async-done(((f32[800,128]{1,0:T(8,128)}), f32[800,128]{1,0:T(8,128)}) %all-reduce.2.cloned.1.call-update) | async-done | bytes 409616 | tf_op jit(solution)/shard_map/psum | solution.py:41
  208.0 0.8 divide_bitcast_fusion
  208.8 0.6 copy.13
  209.5 0.6 broadcast_in_dim.20
  (9 shorter events, 0.1 us)
Async XLA Ops:
  7.2 84.0 %copy-start = (f32[1,800,800]{2,1,0:T(8,128)S(1)}, f32[1,800,800]{2,1,0:T(8,128)}, u32[]{:S(2)}) copy-start(f32[1,800,800]{2,1,0:T(8,128)} %param.9) | copy-start | bytes 7680004
  7.2 80.5 %all-gather.2.cloned.1.call-start = ((), (), s32[]{:S(2)}) async-start(), calls=%async_computation | async-start | bytes 3784704 | tf_op jit(solution)/shard_map/all_gather | solution.py:35
  9.0 199.0 %all-reduce.2.cloned.1.call-start = ((), (), s32[]{:S(2)}) async-start(), calls=%async_computation.1 | async-start | bytes 819200 | tf_op jit(solution)/shard_map/psum | solution.py:41
Sparse Core Ops, SparseCore 0:
  10.1 77.5 all-gather.1
  95.5 112.4 all-reduce.1
where the time goes:
time: 217 us
  waiting for transfers between devices  181 us (83%)
  between operations  16.7 us (8%)
  local copies, waits for them, and re-layouts  13.8 us (6%)
  matrix products  4.2 us (2%)
    psum x1, waiting for transfers between devices, on_device(): summed = lax.psum(partial_value, 'ctr')  113 us
    all_gather x1, waiting for transfers between devices, on_device(): lax.all_gather(amplitudes, 'blk', axis=2, tiled=True)  68.6 us
  transfers between devices with their start and end apart: 2, of which 2 were waited for; matrix products, arithmetic and copies ran while one was open for 3% of the time, Pallas kernels for 0%

commit v1 on v0

--- a/solution.py
+++ b/solution.py
@@ -32,7 +32,12 @@
     ab_block = local.shape[0]
     share = ab_block // lax.axis_size("ctr")
     chosen = lax.dynamic_index_in_dim(
-        lax.all_gather(amplitudes, "blk", axis=2, tiled=True), irrep, 0, keepdims=False
+        jnp.concatenate(
+            lax.all_to_all(jnp.stack([amplitudes] * lax.axis_size("blk")), "blk", 0, 0), axis=2
+        ),
+        irrep,
+        0,
+        keepdims=False,
     )
     partial_value = jnp.dot(
         local, chosen, preferred_element_type=jnp.float32, precision=lax.Precision.HIGHEST

time: 217 us -> 318 us (1.47)
  waiting for transfers between devices: 181 us -> 268 us
  starting transfers between devices: 0.08 us -> 15.6 us
    all_to_all x0 -> x1, waiting for transfers between devices: none -> 160 us  [on_device(): lax.all_to_all(jnp.stack([amplitudes] * lax.axis_size('blk')), 'blk', 0, 0)]
    all_gather x1 -> x0, waiting for transfers between devices: 68.6 us -> none  [on_device(): lax.all_gather(amplitudes, 'blk', axis=2, tiled=True)]
    all_to_all x0 -> x1, starting transfers between devices: none -> 15.5 us  [on_device(): lax.all_to_all(jnp.stack([amplitudes] * lax.axis_size('blk')), 'blk', 0, 0)]
    psum x1, waiting for transfers between devices: 113 us -> 108 us  [on_device(): summed = lax.psum(partial_value, 'ctr')]
  transfers between devices with their start and end apart: 2 -> 2, of which waited for: 2 -> 2; matrix products, arithmetic and copies ran while one was open for 3% -> 1% of each run, Pallas kernels for 0% -> 0%
where the time goes in v1:
time: 318 us
  waiting for transfers between devices  268 us (84%)
  between operations  16.8 us (5%)
  starting transfers between devices  15.6 us (5%)
  local copies, waits for them, and re-layouts  12.7 us (4%)
  matrix products  4.18 us (1%)
    all_to_all x1, waiting for transfers between devices, on_device(): lax.all_to_all(jnp.stack([amplitudes] * lax.axis_size('blk')), 'blk', 0, 0)  160 us
    psum x1, waiting for transfers between devices, on_device(): summed = lax.psum(partial_value, 'ctr')  108 us
    all_to_all x1, starting transfers between devices, on_device(): lax.all_to_all(jnp.stack([amplitudes] * lax.axis_size('blk')), 'blk', 0, 0)  15.5 us
  transfers between devices with their start and end apart: 2, of which 2 were waited for; matrix products, arithmetic and copies ran while one was open for 1% of the time, Pallas kernels for 0%

profile of v1, /device:TPU:32, one launch (start us, length us, event | category | flops | bytes accessed | tf_op | source)
XLA Modules:
  0.0 317.9 jit_solution(12202469258042509234)
XLA Ops:
  7.2 0.0 copy-start
  7.2 1.1 copy.11
  8.2 2.3 stack.2
  10.5 0.0 copy-start.3
  10.5 0.0 copy-start.2
  10.5 0.0 copy-start.1
  10.5 15.5 %all-to-all-start = ((f32[32,8,800,4]{2,1,3,0:T(8,128)}), f32[32,8,800,4]{2,1,3,0:T(8,128)}, u32[]{:S(2)}, u32[]{:S(2)}) async-start(f32[32,8,800,4]{2,1,3,0:T(8,128)} %stack.2), calls=%async_computation | async-start | bytes 7340032 | tf_op jit(solution)/shard_map/all_to_all | solution.py:36
  26.0 0.0 all-reduce.2.cloned.1.call-start
  26.1 0.0 copy-done.3
  26.1 0.6 dynamic_slice.10
  29.4 0.0 copy-done.2
  29.4 0.8 gather_fusion
  30.2 0.8 gather_fusion.1
  31.0 0.0 copy-done.1
  31.0 1.2 gather_fusion.3
  32.3 1.2 gather_fusion.2
  33.5 159.9 %all-to-all-done = f32[32,8,800,4]{2,1,3,0:T(8,128)} async-done(((f32[32,8,800,4]{2,1,3,0:T(8,128)}), f32[32,8,800,4]{2,1,3,0:T(8,128)}, u32[]{:S(2)}, u32[]{:S(2)}) %all-to-all-start) | async-done | bytes 3276832 | tf_op jit(solution)/shard_map/all_to_all | solution.py:36
  193.4 2.4 constant_dynamic-slice_fusion.1
  195.7 1.1 copy.12
  196.8 0.0 copy-done
  196.8 4.2 %fusion.2 = f32[800,128]{1,0:T(8,128)} fusion(f32[1,800,800]{2,1,0:T(8,128)S(1)} %copy-done, f32[1,800,128]{2,1,0:T(8,128)} %copy.12), kind=kOutput, calls=%fused_computation.6 | convolution fusion | flops 983040000 | bytes 3379200 | tf_op jit(solution)/shard_map/dot_general | solution.py:42
  201.0 0.0 all-reduce.2.cloned.1.call-update
  201.1 107.9 %all-reduce.2.cloned.1.call-done = f32[800,128]{1,0:T(8,128)} async-done(((f32[800,128]{1,0:T(8,128)}), f32[800,128]{1,0:T(8,128)}) %all-reduce.2.cloned.1.call-update) | async-done | bytes 409616 | tf_op jit(solution)/shard_map/psum | solution.py:46
  309.0 0.8 divide_bitcast_fusion
  309.8 0.6 copy.13
  310.5 0.6 broadcast_in_dim.20
  (9 shorter events, 0.1 us)
Async XLA Ops:
  7.2 189.7 %copy-start = (f32[1,800,800]{2,1,0:T(8,128)S(1)}, f32[1,800,800]{2,1,0:T(8,128)}, u32[]{:S(2)}) copy-start(f32[1,800,800]{2,1,0:T(8,128)} %param.9) | copy-start | bytes 7680004
  10.5 15.6 %copy-start.3 = (s32[32]{0:T(128)S(1)}, s32[32]{0:T(128)}, u32[]{:S(2)}) copy-start(s32[32]{0:T(128)} %param.11) | copy-start | bytes 388
  10.5 18.9 %copy-start.2 = (f32[320]{0:T(512)S(1)}, f32[320]{0:T(512)}, u32[]{:S(2)}) copy-start(f32[320]{0:T(512)} %param.12) | copy-start | bytes 3844
  10.5 20.5 %copy-start.1 = (f32[32]{0:T(128)S(1)}, f32[32]{0:T(128)}, u32[]{:S(2)}) copy-start(f32[32]{0:T(128)} %param.13) | copy-start | bytes 388
  10.5 182.9 %all-to-all-start = ((f32[32,8,800,4]{2,1,3,0:T(8,128)}), f32[32,8,800,4]{2,1,3,0:T(8,128)}, u32[]{:S(2)}, u32[]{:S(2)}) async-start(f32[32,8,800,4]{2,1,3,0:T(8,128)} %stack.2), calls=%async_computation | async-start | bytes 7340032 | tf_op jit(solution)/shard_map/all_to_all | solution.py:36
  26.0 282.9 %all-reduce.2.cloned.1.call-start = ((), (), s32[]{:S(2)}) async-start(), calls=%async_computation.1 | async-start | bytes 819200 | tf_op jit(solution)/shard_map/psum | solution.py:46
Sparse Core Ops, SparseCore 0:
  201.2 107.7 all-reduce.1

commit v2 on v0

--- a/solution.py
+++ b/solution.py
@@ -38,7 +38,7 @@
         local, chosen, preferred_element_type=jnp.float32, precision=lax.Precision.HIGHEST
     )
     offset = lax.axis_index("ctr") * share
-    summed = lax.psum(partial_value, "ctr")
+    summed = jnp.sum(lax.all_gather(partial_value, "ctr"), axis=0)
     mine = lax.dynamic_slice_in_dim(summed, offset, share, 0)
     denom = denominator(
         block, groups, ab_block, offset, share, partial_value.shape[1], vir_energy, occ_energy

time: 217 us -> 183 us (0.84)
  the two profiles are of different devices: /device:TPU:32 before, /device:TPU:1 now
where the time goes in v2:
time: 183 us
  waiting for transfers between devices  147 us (80%)
  between operations  16.8 us (9%)
  local copies, waits for them, and re-layouts  11.7 us (6%)
  matrix products  4.21 us (2%)
  other arithmetic  3.41 us (2%)
    all_gather x1, waiting for transfers between devices, on_device(): lax.all_gather(amplitudes, 'blk', axis=2, tiled=True)  76.6 us
    all_gather x1, waiting for transfers between devices, on_device(): summed = jnp.sum(lax.all_gather(partial_value, 'ctr'), axis=0)  70.3 us
    dot_general x1, matrix products, on_device(): jnp.dot(local, chosen, preferred_element_type=jnp.float32, precision=lax....  4.21 us
  transfers between devices with their start and end apart: 2, of which 2 were waited for; matrix products, arithmetic and copies ran while one was open for 3% of the time, Pallas kernels for 0%

profile of v2, /device:TPU:1, one launch (start us, length us, event | category | flops | bytes accessed | tf_op | source)
XLA Modules:
  0.0 183.2 jit_solution(4115591407292680307)
XLA Ops:
  7.2 0.0 copy-start
  7.2 0.0 all-gather.4.cloned.1.call-start
  7.2 1.7 copy.8
  8.9 0.0 all-gather.4.cloned.1.call-update
  8.9 0.0 all-gather.6.cloned.1.call-start
  9.0 1.2 dynamic_slice.10
  12.9 0.0 copy-start.2
  12.9 76.6 %all-gather.4.cloned.1.call-done = f32[8,800,128]{1,0,2:T(8,128)} async-done(((f32[8,800,4]{1,0,2:T(8,128)}), f32[8,800,128]{1,0,2:T(8,128)}) %all-gather.4.cloned.1.call-update) | async-done | bytes 3276816 | tf_op jit(solution)/shard_map/all_gather | solution.py:35
  89.5 2.4 %constant_dynamic-slice_fusion.1 = f32[1,800,128]{1,0,2:T(1,128)S(1)} fusion(f32[8,800,128]{1,0,2:T(8,128)} %all-gather.4.cloned.1.call-done, s32[]{:T(128)S(6)} %select_n.74), kind=kLoop, calls=%fused_computation.47 | loop fusion | bytes 819204 | tf_op jit(solution)/shard_map/jit(dynamic_index_in_dim)/dynamic_slice | solution.py:34
  91.8 0.0 copy-start.1
  91.8 1.1 copy.10
  92.9 0.0 copy-done
  92.9 4.2 %fusion.2 = f32[800,128]{1,0:T(8,128)} fusion(f32[1,800,800]{2,1,0:T(8,128)S(1)} %copy-done, f32[1,800,128]{2,1,0:T(8,128)} %copy.10), kind=kOutput, calls=%fused_computation.6 | convolution fusion | flops 983040000 | bytes 3379200 | tf_op jit(solution)/shard_map/dot_general | solution.py:37
  97.2 0.0 all-gather.6.cloned.1.call-update
  97.2 0.0 copy-done.2
  97.2 0.8 gather_fusion
  98.1 0.8 gather_fusion.1
  98.9 0.0 copy-done.1
  98.9 1.2 gather_fusion.3
  100.1 1.2 gather_fusion.2
  101.4 70.3 %all-gather.6.cloned.1.call-done = f32[12800,128]{1,0:T(8,128)} async-done(((f32[800,128]{1,0:T(8,128)}), f32[12800,128]{1,0:T(8,128)}) %all-gather.6.cloned.1.call-update) | async-done | bytes 6553616 | tf_op jit(solution)/shard_map/all_gather | solution.py:41
  171.8 3.2 %reduce_sum.9 = f32[800,128]{1,0:T(8,128)S(1)} reduce(f32[16,800,128]{2,1,0:T(8,128)} %bitcast.12, f32[]{:T(128)} %constant.128.clone.1), dimensions={0}, to_apply=%region_0.1 | reduce | flops 1536000 | bytes 6963204 | tf_op jit(solution)/shard_map/reduce_sum | solution.py:41
  175.0 0.1 subtract_divide_fusion
  175.1 0.6 broadcast_in_dim.21
  175.7 0.6 broadcast_in_dim.20
  (9 shorter events, 0.1 us)
Async XLA Ops:
  7.2 85.8 %copy-start = (f32[1,800,800]{2,1,0:T(8,128)S(1)}, f32[1,800,800]{2,1,0:T(8,128)}, u32[]{:S(2)}) copy-start(f32[1,800,800]{2,1,0:T(8,128)} %param.9) | copy-start | bytes 7680004
  7.2 82.3 %all-gather.4.cloned.1.call-start = ((), (), s32[]{:S(2)}) async-start(), calls=%async_computation | async-start | bytes 3784704 | tf_op jit(solution)/shard_map/all_gather | solution.py:35
  8.9 162.8 %all-gather.6.cloned.1.call-start = ((), (), s32[]{:S(2)}) async-start(), calls=%async_computation.1 | async-start | bytes 6963200 | tf_op jit(solution)/shard_map/all_gather | solution.py:41
  12.9 84.4 %copy-start.2 = (f32[320]{0:T(512)S(1)}, f32[320]{0:T(512)}, u32[]{:S(2)}) copy-start(f32[320]{0:T(512)} %param.12) | copy-start | bytes 3844
  91.8 7.1 %copy-start.1 = (f32[32]{0:T(128)S(1)}, f32[32]{0:T(128)}, u32[]{:S(2)}) copy-start(f32[32]{0:T(128)} %param.13) | copy-start | bytes 388
Sparse Core Ops, SparseCore 0:
  10.1 79.2 all-gather.3
  97.3 74.4 all-gather.5
